TPU v7x, 32 devices: a whole 2x2x4 slice. The times are simulated.
32 devices in a mesh: passage: 2 (over x), brick: 16 (over z, y, core).
Axes of the slice: x: 2, y: 2, z: 4, core: 2. Of those that a mesh axis runs over, the one named last changes fastest.
Arguments:
- jac_blocks: bfloat16 [2, 25, 16, 8192], P('passage', None, None, 'brick'), may hold values from -6 to 6
- psi_start: float32 [2, 10, 16, 64, 128], P('passage', None, 'brick'), may hold values from -6 to 6
- source: float32 [2, 10, 16, 64, 128], P('passage', None, 'brick'), may hold values from -6 to 6
- pseudo_step: float32 [2, 16, 64, 128], P('passage', 'brick'), may hold values from 0.1 to 0.4
- dissipation: float32 [2, 16, 64, 128], P('passage', 'brick'), may hold values from 0.04 to 0.15
- freq_volume: float32 [2, 16, 64, 128], P('passage', 'brick'), may hold values from 0.2 to 2
- normals: float32 [2, 3, 16, 64], P('passage', None, 'brick'), may hold values from -6 to 6
- face_owner: int32 [2, 1024, 1], P('passage', 'brick'), may hold values from 0 to 15; in each aligned block of 64 rows (0 to 63, 64 to 127, ..., all dimensions but the last counted through in order) at most 16 rows name the same one
- face_slot: int32 [2, 1024], P('passage', 'brick'), may hold values from 0 to 255
Outputs:
- adjoint: float32 [2, 10, 16, 64, 128], P('passage', None, 'brick')
- sensitivity: float32 [2, 6, 4096], P('passage', None, 'brick')
Inputs may be any that keep to these rules, and one draw needn't show every extreme that they name: `face_owner`: in the 64 faces of one device (aligned blocks of the rows), no brick is named by more than 16 faces, and in some block some brick is named by exactly 16.
All inputs are finite; a program needn't handle non-finite values.
Results may differ from a plain program's by a relative error of at most 0.0003.
Values may be sent and summed in bfloat16 or wider, within the bound.
A program may use at most 64 MiB of HBM per device.

v0:
```python
import math
import jax
import jax.numpy as jnp
from jax import lax
from jax.sharding import PartitionSpec as P

NODE_DEV = 256
SWEEPS = 2
ND = 1
BLADES = 36


def padded(value, sides, width, wrap):
    for axis, dim in sides:
        peers, length = (lax.axis_size(axis), value.shape[dim])
        up = [(i, (i + 1) % peers) for i in range(peers if wrap else peers - 1)]
        down = [(j, i) for i, j in up]
        last = lax.slice_in_dim(value, length - width, length, axis=dim)
        initial = lax.slice_in_dim(value, 0, width, axis=dim)
        before = lax.ppermute(last, axis, up)
        after = lax.ppermute(initial, axis, down)
        value = jnp.concatenate([before, value, after], axis=dim)
    return value


def rotate(rim, turn):
    cosine = math.cos(turn)
    sine = math.sin(turn)
    real_part = rim[:, :5]
    imag_part = rim[:, 5:]
    return jnp.concatenate(
        [real_part * cosine - imag_part * sine, real_part * sine + imag_part * cosine], axis=1
    )


def transpose_apply(tiles, diff):
    total_real = jnp.zeros_like(diff[:, :5])
    total_imag = jnp.zeros_like(diff[:, :5])
    for row_index in range(5):
        column = tiles[:, row_index * 5 : row_index * 5 + 5].astype(jnp.float32)
        total_real = total_real + column * diff[:, row_index : row_index + 1]
        total_imag = total_imag + column * diff[:, 5 + row_index : 6 + row_index]
    return jnp.concatenate([total_real, total_imag], axis=1)


def advance(
    state,
    source,
    pseudo_step,
    dissipation,
    freq_volume,
    convect_fn,
    cycle_index,
    passes,
    phase_angle,
):
    padded_i = padded(state, (("brick", 2),), 1, False)
    padded_j = padded(state.astype(jnp.bfloat16), (("passage", 3),), 1, True).astype(state.dtype)
    below_rim = padded_j[:, :, :, :1]
    above_rim = padded_j[:, :, :, -1:]
    below_rim = jnp.where(cycle_index == 0, rotate(below_rim, -phase_angle), below_rim)
    above_rim = jnp.where(cycle_index == passes - 1, rotate(above_rim, phase_angle), above_rim)
    fixed_j = jnp.concatenate([below_rim, state, above_rim], axis=3)
    padded_k = jnp.pad(state, ((0, 0), (0, 0), (0, 0), (0, 0), (1, 1)))
    beside = padded_i[:, :, 2:] + padded_i[:, :, :-2]
    beside = beside + fixed_j[:, :, :, 2:] + fixed_j[:, :, :, :-2]
    beside = beside + padded_k[..., 2:] + padded_k[..., :-2]
    diff = 0.5 * (padded_i[:, :, 2:] - padded_i[:, :, :-2])
    convect = convect_fn(diff)
    omega = freq_volume[:, None]
    spin = jnp.concatenate([omega * state[:, 5:], -omega * state[:, :5]], axis=1)
    resid = convect + spin + dissipation[:, None] * (6.0 * state - beside) - source
    return state - pseudo_step[:, None] * resid


def body(
    jac_blocks,
    psi_start,
    source,
    pseudo_step,
    dissipation,
    freq_volume,
    normals,
    face_owner,
    face_slot,
):
    passes = lax.axis_size("passage")
    cycle_index = lax.axis_index("passage")
    bricks = lax.axis_size("brick")
    planes = psi_start.shape[2]
    width_j = psi_start.shape[3]
    width_k = psi_start.shape[4]
    phase_angle = 2.0 * math.pi * ND * passes / BLADES
    relaid = lax.all_to_all(jac_blocks, "brick", split_axis=2, concat_axis=3, tiled=True)
    tiles = relaid.reshape(1, 25, planes, width_j, width_k)

    def convect_fn(diff):
        return transpose_apply(tiles, diff)

    state = psi_start
    for sweep in range(SWEEPS):
        state = advance(
            state,
            source,
            pseudo_step,
            dissipation,
            freq_volume,
            convect_fn,
            cycle_index,
            passes,
            phase_angle,
        )
    wall_state = state[0, :, :, :, 0]
    face_normals = normals[0]
    values = jnp.concatenate(
        [face_normals * wall_state[1:4], face_normals * wall_state[6:9]], axis=0
    )
    values = values.reshape(6, planes * width_j)
    owners = face_owner[0, :, 0]
    slots = face_slot[0]
    node_ids = owners * NODE_DEV + slots
    local_terms = jnp.zeros((6, NODE_DEV * bricks), jnp.float32).at[:, node_ids].add(values)
    summed = lax.psum_scatter(local_terms, "brick", scatter_dimension=1, tiled=True)
    sensitivity = summed[None]
    return (state, sensitivity)


def solution(mesh):
    placed = (
        P("passage", None, None, "brick"),
        P("passage", None, "brick", None, None),
        P("passage", None, "brick", None, None),
        P("passage", "brick", None, None),
        P("passage", "brick", None, None),
        P("passage", "brick", None, None),
        P("passage", None, "brick", None),
        P("passage", "brick", None),
        P("passage", "brick"),
    )
    return jax.shard_map(
        body,
        mesh=mesh,
        in_specs=placed,
        out_specs=(P("passage", None, "brick", None, None), P("passage", None, "brick")),
        check_vma=False,
    )
```

profile of v0, /device:TPU:0, one launch (start us, length us, event | category | flops | bytes accessed | tf_op | source)
XLA Modules:
  0.0 128.0 jit_solution(5724360956886795302)
XLA Ops:
  7.2 0.0 copy-start
  7.2 0.0 copy-start.3
  7.2 0.0 copy-start.7
  7.2 0.0 copy-start.8
  7.2 2.5 %collective-permute-start.1 = (f32[1,10,1,64,128]{4,3,1,2,0:T(8,128)}, f32[1,10,1,64,128]{4,3,1,2,0:T(8,128)S(1)}, u32[]{:S(2)}, u32[]{:S(2)}) collective-permute-start(f32[1,10,1,64,128]{4,3,1,2,0:T(8,128)} %bitcast.71), channel_id=1, source_target_pairs={{0,1},{1,2},{2,3},{3,4},{4,5},{5,6},{6,7},{7,8},{8,9},{9,10},{10,1... | collective-permute-start | bytes 983048 | tf_op jit(solution)/shard_map/ppermute | solution.py:20
  9.8 1.3 %collective-permute-start = (f32[1,10,1,64,128]{4,3,1,2,0:T(8,128)}, f32[1,10,1,64,128]{4,3,1,2,0:T(8,128)S(1)}, u32[]{:S(2)}, u32[]{:S(2)}) collective-permute-start(f32[1,10,1,64,128]{4,3,1,2,0:T(8,128)} %bitcast.72), channel_id=1, source_target_pairs={{1,0},{2,1},{3,2},{4,3},{5,4},{6,5},{7,6},{8,7},{9,8},{10,9},{11,1... | collective-permute-start | bytes 983048 | tf_op jit(solution)/shard_map/ppermute | solution.py:21
  11.1 1.0 bitcast_convert_fusion
  12.1 2.4 %collective-permute-start.2 = (bf16[1,10,1,1,128]{4,3,1,2,0:T(2,128)(2,1)S(1)}, bf16[1,10,1,1,128]{4,3,1,2,0:T(2,128)(2,1)S(1)}, u32[]{:S(2)}, u32[]{:S(2)}) collective-permute-start(bf16[1,10,1,1,128]{4,3,1,2,0:T(2,128)(2,1)S(1)} %get-tuple-element.64), channel_id=1, source_target_pairs={{0,16},{16,0},{1,17},{17,1},{2,18},{18,2},{3,19},{19,3},{4,20},{20... | collective-permute-start | bytes 7688 | tf_op jit(solution)/shard_map/ppermute | solution.py:20
  14.5 0.1 collective-permute-start.3
  14.5 2.0 %copy.66 = bf16[1,25,16,512]{3,1,0,2:T(8,128)(2,1)} copy(bf16[1,25,16,512]{3,2,1,0:T(8,128)(2,1)} %param.9) | data formatting | bytes 819200 | tf_op args[0]
  16.6 8.9 %all-to-all-start = ((bf16[1,25,16,512]{3,1,0,2:T(8,128)(2,1)}), bf16[1,25,16,512]{3,1,0,2:T(8,128)(2,1)S(1)}, u32[]{:S(2)}, u32[]{:S(2)}) async-start(bf16[1,25,16,512]{3,1,0,2:T(8,128)(2,1)} %copy.66), calls=%async_computation | async-start | bytes 1048576 | tf_op jit(solution)/shard_map/all_to_all | solution.py:94
  25.5 0.0 reduce-scatter.2.cloned.1.call-start
  25.6 0.0 copy-done.3
  25.6 0.0 copy-done
  25.6 0.0 copy-done.7
  25.6 0.0 copy-done.8
  25.7 0.0 collective-permute-done.2
  25.7 0.0 collective-permute-done.3
  25.8 0.0 collective-permute-done.1
  25.8 0.0 collective-permute-done
  25.8 0.0 copy-start.1
  25.8 0.0 copy-start.4
  25.9 0.0 copy-start.5
  25.9 13.9 %all-to-all-done = bf16[1,25,16,512]{3,1,0,2:T(8,128)(2,1)S(1)} async-done(((bf16[1,25,16,512]{3,1,0,2:T(8,128)(2,1)}), bf16[1,25,16,512]{3,1,0,2:T(8,128)(2,1)S(1)}, u32[]{:S(2)}, u32[]{:S(2)}) %all-to-all-start) | async-done | bytes 409632 | tf_op jit(solution)/shard_map/all_to_all | solution.py:94
  39.8 0.2 copy.67
  40.0 0.2 reshape.329
  40.3 0.1 fusion.29
  40.4 0.1 fusion.25
  40.5 0.3 fusion.50
  40.8 1.6 %collective-permute-start.6 = (bf16[1,10,1,1,128]{4,3,1,2,0:T(2,128)(2,1)S(1)}, bf16[1,10,1,1,128]{4,3,1,2,0:T(2,128)(2,1)S(1)}, u32[]{:S(2)}, u32[]{:S(2)}) collective-permute-start(bf16[1,10,1,1,128]{4,3,1,2,0:T(2,128)(2,1)S(1)} %get-tuple-element.62), channel_id=1, source_target_pairs={{0,16},{16,0},{1,17},{17,1},{2,18},{18,2},{3,19},{19,3},{4,20},{20... | collective-permute-start | bytes 7688 | tf_op jit(solution)/shard_map/ppermute | solution.py:20
  42.4 0.5 collective-permute-start.7
  42.9 1.5 %collective-permute-start.5 = (f32[1,10,1,64,128]{4,3,1,2,0:T(8,128)S(1)}, f32[1,10,1,64,128]{4,3,1,2,0:T(8,128)S(1)}, u32[]{:S(2)}, u32[]{:S(2)}) collective-permute-start(f32[1,10,1,64,128]{4,3,1,2,0:T(8,128)S(1)} %get-tuple-element.21), channel_id=1, source_target_pairs={{0,1},{1,2},{2,3},{3,4},{4,5},{5,6},{6,7},{7,8},{8,9},{9,10},{10,1... | collective-permute-start | bytes 983048 | tf_op jit(solution)/shard_map/ppermute | solution.py:20
  44.5 1.3 %collective-permute-start.4 = (f32[1,10,1,64,128]{4,3,1,2,0:T(8,128)S(1)}, f32[1,10,1,64,128]{4,3,1,2,0:T(8,128)S(1)}, u32[]{:S(2)}, u32[]{:S(2)}) collective-permute-start(f32[1,10,1,64,128]{4,3,1,2,0:T(8,128)S(1)} %get-tuple-element.21), channel_id=1, source_target_pairs={{1,0},{2,1},{3,2},{4,3},{5,4},{6,5},{7,6},{8,7},{9,8},{10,9},{11,1... | collective-permute-start | bytes 983048 | tf_op jit(solution)/shard_map/ppermute | solution.py:21
  45.8 0.0 collective-permute-done.6
  45.8 0.2 collective-permute-done.7
  46.1 0.0 collective-permute-done.5
  46.1 2.3 %collective-permute-done.4 = f32[1,10,1,64,128]{4,3,1,2,0:T(8,128)S(1)} collective-permute-done((f32[1,10,1,64,128]{4,3,1,2,0:T(8,128)S(1)}, f32[1,10,1,64,128]{4,3,1,2,0:T(8,128)S(1)}, u32[]{:S(2)}, u32[]{:S(2)}) %collective-permute-start.4) | collective-permute-done | bytes 327712 | tf_op jit(solution)/shard_map/ppermute | solution.py:21
  48.5 0.0 copy-start.6
  48.5 0.1 fusion.33
  48.6 0.1 fusion.37
  48.7 0.4 fusion.17
  49.1 0.0 copy-start.2
  49.1 0.1 slice_reduce_fusion.1
  49.3 0.1 copy.84
  49.4 2.2 %scatter_custom_fusion = f32[6,4096]{0,1:T(8,128)} fusion(s32[64]{0:T(128)S(1)} %fusion.49, f32[]{:T(128)} %constant.11.clone.1, f32[6,1,64]{0,2,1:T(8,128)S(1)} %copy.84), kind=kCustom, calls=%fused_computation.1 | custom fusion | flops 384 | bytes 131076 | tf_op jit(solution)/shard_map/scatter-add | solution.py:122
  51.6 0.0 reduce-scatter.2.cloned.1.call-update
  51.6 68.0 %reduce-scatter.2.cloned.1.call-done = f32[6,256]{0,1:T(8,128)} async-done(((f32[6,4096]{0,1:T(8,128)}), f32[6,256]{0,1:T(8,128)}) %reduce-scatter.2.cloned.1.call-update) | async-done | bytes 6160 | tf_op jit(solution)/shard_map/reduce_scatter | solution.py:123
  119.6 1.6 %copy.82 = f32[1,6,256]{2,0,1:T(1,128)} copy(f32[1,6,256]{1,2,0:T(8,128)} %bitcast.82) | data formatting | bytes 12288
  (24 shorter events, 0.4 us)
Async XLA Ops:
  7.2 18.4 %copy-start = (f32[1,10,1,64,128]{4,3,2,1,0:T(8,128)S(1)}, f32[1,10,1,64,128]{4,3,2,1,0:T(8,128)}, u32[]{:S(2)}) copy-start(f32[1,10,1,64,128]{4,3,2,1,0:T(8,128)} %param.10) | copy-start | bytes 983044
  7.2 18.4 %copy-start.3 = (f32[1,1,64,128]{3,2,1,0:T(8,128)S(1)}, f32[1,1,64,128]{3,2,1,0:T(8,128)}, u32[]{:S(2)}) copy-start(f32[1,1,64,128]{3,2,1,0:T(8,128)} %param.14) | copy-start | bytes 98308
  7.2 18.4 %copy-start.7 = (s32[1,64]{1,0:T(1,128)S(1)}, s32[1,64]{1,0:T(1,128)}, u32[]{:S(2)}) copy-start(s32[1,64]{1,0:T(1,128)} %param.17) | copy-start | bytes 772
  7.2 18.4 %copy-start.8 = (s32[1,64,1]{1,2,0:T(1,128)S(1)}, s32[1,64,1]{1,2,0:T(1,128)}, u32[]{:S(2)}) copy-start(s32[1,64,1]{1,2,0:T(1,128)} %param.16) | copy-start | bytes 772
  7.2 18.6 %collective-permute-start.1 = (f32[1,10,1,64,128]{4,3,1,2,0:T(8,128)}, f32[1,10,1,64,128]{4,3,1,2,0:T(8,128)S(1)}, u32[]{:S(2)}, u32[]{:S(2)}) collective-permute-start(f32[1,10,1,64,128]{4,3,1,2,0:T(8,128)} %bitcast.71), channel_id=1, source_target_pairs={{0,1},{1,2},{2,3},{3,4},{4,5},{5,6},{6,7},{7,8},{8,9},{9,10},{10,1... | collective-permute-start | bytes 983048 | tf_op jit(solution)/shard_map/ppermute | solution.py:20
  9.8 16.0 %collective-permute-start = (f32[1,10,1,64,128]{4,3,1,2,0:T(8,128)}, f32[1,10,1,64,128]{4,3,1,2,0:T(8,128)S(1)}, u32[]{:S(2)}, u32[]{:S(2)}) collective-permute-start(f32[1,10,1,64,128]{4,3,1,2,0:T(8,128)} %bitcast.72), channel_id=1, source_target_pairs={{1,0},{2,1},{3,2},{4,3},{5,4},{6,5},{7,6},{8,7},{9,8},{10,9},{11,1... | collective-permute-start | bytes 983048 | tf_op jit(solution)/shard_map/ppermute | solution.py:21
  12.1 13.6 %collective-permute-start.2 = (bf16[1,10,1,1,128]{4,3,1,2,0:T(2,128)(2,1)S(1)}, bf16[1,10,1,1,128]{4,3,1,2,0:T(2,128)(2,1)S(1)}, u32[]{:S(2)}, u32[]{:S(2)}) collective-permute-start(bf16[1,10,1,1,128]{4,3,1,2,0:T(2,128)(2,1)S(1)} %get-tuple-element.64), channel_id=1, source_target_pairs={{0,16},{16,0},{1,17},{17,1},{2,18},{18,2},{3,19},{19,3},{4,20},{20... | collective-permute-start | bytes 7688 | tf_op jit(solution)/shard_map/ppermute | solution.py:20
  14.5 11.2 %collective-permute-start.3 = (bf16[1,10,1,1,128]{4,3,1,2,0:T(2,128)(2,1)S(1)}, bf16[1,10,1,1,128]{4,3,1,2,0:T(2,128)(2,1)S(1)}, u32[]{:S(2)}, u32[]{:S(2)}) collective-permute-start(bf16[1,10,1,1,128]{4,3,1,2,0:T(2,128)(2,1)S(1)} %get-tuple-element.65), channel_id=1, source_target_pairs={{16,0},{0,16},{17,1},{1,17},{18,2},{2,18},{19,3},{3,19},{20,4},{4,... | collective-permute-start | bytes 7688 | tf_op jit(solution)/shard_map/ppermute | solution.py:21
  16.6 23.2 %all-to-all-start = ((bf16[1,25,16,512]{3,1,0,2:T(8,128)(2,1)}), bf16[1,25,16,512]{3,1,0,2:T(8,128)(2,1)S(1)}, u32[]{:S(2)}, u32[]{:S(2)}) async-start(bf16[1,25,16,512]{3,1,0,2:T(8,128)(2,1)} %copy.66), calls=%async_computation | async-start | bytes 1048576 | tf_op jit(solution)/shard_map/all_to_all | solution.py:94
  25.5 94.1 %reduce-scatter.2.cloned.1.call-start = ((), (), s32[]{:S(2)}) async-start(), calls=%async_computation.2 | async-start | bytes 2228224 | tf_op jit(solution)/shard_map/reduce_scatter | solution.py:123
  25.8 14.6 %copy-start.1 = (f32[1,10,1,64,128]{4,3,2,1,0:T(8,128)S(1)}, f32[1,10,1,64,128]{4,3,2,1,0:T(8,128)}, u32[]{:S(2)}) copy-start(f32[1,10,1,64,128]{4,3,2,1,0:T(8,128)} %param.11) | copy-start | bytes 983044
  25.8 14.6 %copy-start.4 = (f32[1,1,64,128]{3,2,1,0:T(8,128)S(1)}, f32[1,1,64,128]{3,2,1,0:T(8,128)}, u32[]{:S(2)}) copy-start(f32[1,1,64,128]{3,2,1,0:T(8,128)} %param.13) | copy-start | bytes 98308
  25.9 14.6 %copy-start.5 = (f32[1,1,64,128]{3,2,1,0:T(8,128)S(1)}, f32[1,1,64,128]{3,2,1,0:T(8,128)}, u32[]{:S(2)}) copy-start(f32[1,1,64,128]{3,2,1,0:T(8,128)} %param.12) | copy-start | bytes 98308
  40.8 4.9 %collective-permute-start.6 = (bf16[1,10,1,1,128]{4,3,1,2,0:T(2,128)(2,1)S(1)}, bf16[1,10,1,1,128]{4,3,1,2,0:T(2,128)(2,1)S(1)}, u32[]{:S(2)}, u32[]{:S(2)}) collective-permute-start(bf16[1,10,1,1,128]{4,3,1,2,0:T(2,128)(2,1)S(1)} %get-tuple-element.62), channel_id=1, source_target_pairs={{0,16},{16,0},{1,17},{17,1},{2,18},{18,2},{3,19},{19,3},{4,20},{20... | collective-permute-start | bytes 7688 | tf_op jit(solution)/shard_map/ppermute | solution.py:20
  42.4 3.6 %collective-permute-start.7 = (bf16[1,10,1,1,128]{4,3,1,2,0:T(2,128)(2,1)S(1)}, bf16[1,10,1,1,128]{4,3,1,2,0:T(2,128)(2,1)S(1)}, u32[]{:S(2)}, u32[]{:S(2)}) collective-permute-start(bf16[1,10,1,1,128]{4,3,1,2,0:T(2,128)(2,1)S(1)} %get-tuple-element.63), channel_id=1, source_target_pairs={{16,0},{0,16},{17,1},{1,17},{18,2},{2,18},{19,3},{3,19},{20,4},{4,... | collective-permute-start | bytes 7688 | tf_op jit(solution)/shard_map/ppermute | solution.py:21
  42.9 3.1 %collective-permute-start.5 = (f32[1,10,1,64,128]{4,3,1,2,0:T(8,128)S(1)}, f32[1,10,1,64,128]{4,3,1,2,0:T(8,128)S(1)}, u32[]{:S(2)}, u32[]{:S(2)}) collective-permute-start(f32[1,10,1,64,128]{4,3,1,2,0:T(8,128)S(1)} %get-tuple-element.21), channel_id=1, source_target_pairs={{0,1},{1,2},{2,3},{3,4},{4,5},{5,6},{6,7},{7,8},{8,9},{9,10},{10,1... | collective-permute-start | bytes 983048 | tf_op jit(solution)/shard_map/ppermute | solution.py:20
  44.5 4.0 %collective-permute-start.4 = (f32[1,10,1,64,128]{4,3,1,2,0:T(8,128)S(1)}, f32[1,10,1,64,128]{4,3,1,2,0:T(8,128)S(1)}, u32[]{:S(2)}, u32[]{:S(2)}) collective-permute-start(f32[1,10,1,64,128]{4,3,1,2,0:T(8,128)S(1)} %get-tuple-element.21), channel_id=1, source_target_pairs={{1,0},{2,1},{3,2},{4,3},{5,4},{6,5},{7,6},{8,7},{9,8},{10,9},{11,1... | collective-permute-start | bytes 983048 | tf_op jit(solution)/shard_map/ppermute | solution.py:21
  48.5 0.7 copy-start.6
  49.1 2.5 %copy-start.2 = (f32[1,10,1,64,128]{4,3,1,2,0:T(8,128)}, f32[1,10,1,64,128]{4,3,1,2,0:T(8,128)S(1)}, u32[]{:S(2)}) copy-start(f32[1,10,1,64,128]{4,3,1,2,0:T(8,128)S(1)} %fusion.17) | copy-start | bytes 983044
Sparse Core Ops, SparseCore 0:
  51.7 67.8 reduce-scatter.1
where the time goes:
time: 128 us
  waiting for transfers between devices  84.5 us (66%)
  starting transfers between devices  20.1 us (16%)
  between operations  14.5 us (11%)
  other arithmetic  4.52 us (4%)
  local copies, waits for them, and re-layouts  4.46 us (3%)
    reduce_scatter x1, waiting for transfers between devices, body(): lax.psum_scatter(local_terms, 'brick', scatter_dimension=1, tiled=True)  68 us
    all_to_all x1, waiting for transfers between devices, body(): lax.all_to_all(jac_blocks, 'brick', split_axis=2, concat_axis=3, tiled=True)  13.9 us
    all_to_all x1, starting transfers between devices, body(): lax.all_to_all(jac_blocks, 'brick', split_axis=2, concat_axis=3, tiled=True)  8.92 us
    ppermute x4, starting transfers between devices, padded(): before = lax.ppermute(last, axis, up)  7.99 us
    unnamed x20, local copies, waits for them, and re-layouts  3.67 us
    ppermute x4, starting transfers between devices, padded(): after = lax.ppermute(initial, axis, down)  3.2 us
    ppermute x4, waiting for transfers between devices, padded(): after = lax.ppermute(initial, axis, down)  2.58 us
  transfers between devices with their start and end apart: 10, of which 4 were waited for; matrix products, arithmetic and copies ran while one was open for 3% of the time, Pallas kernels for 0%

commit v1 on v0

--- a/solution.py
+++ b/solution.py
@@ -91,7 +91,12 @@
     width_j = psi_start.shape[3]
     width_k = psi_start.shape[4]
     phase_angle = 2.0 * math.pi * ND * passes / BLADES
-    relaid = lax.all_to_all(jac_blocks, "brick", split_axis=2, concat_axis=3, tiled=True)
+    relaid = jnp.concatenate(
+        lax.all_to_all(
+            jnp.stack(jnp.split(jac_blocks, lax.axis_size("brick"), axis=2)), "brick", 0, 0
+        ),
+        axis=3,
+    )
     tiles = relaid.reshape(1, 25, planes, width_j, width_k)
 
     def convect_fn(diff):

time: 128 us -> 135 us (1.055)
  local copies, waits for them, and re-layouts: 4.46 us -> 16.1 us
  waiting for transfers between devices: 84.5 us -> 79.1 us
    unnamed x20 -> x34, local copies, waits for them, and re-layouts: 3.67 us -> 10.7 us
    all_to_all x1, waiting for transfers between devices: 13.9 us -> 8.77 us  [body(): lax.all_to_all(jnp.stack(jnp.split(jac_blocks, lax.axis_size('brick'), ax...]
    split x0 -> x1, local copies, waits for them, and re-layouts: none -> 3.97 us  [body(): jnp.split(jac_blocks, lax.axis_size('brick'), axis=2)]
    reduce_scatter x1, waiting for transfers between devices: 68 us -> 64.2 us  [body(): lax.psum_scatter(local_terms, 'brick', scatter_dimension=1, tiled=True)]
    ppermute x4, waiting for transfers between devices: 0.01 us -> 3.08 us  [padded(): before = lax.ppermute(last, axis, up)]
  transfers between devices with their start and end apart: 10 -> 10, of which waited for: 4 -> 6; matrix products, arithmetic and copies ran while one was open for 3% -> 10% of each run, Pallas kernels for 0% -> 0%
where the time goes in v1:
time: 135 us; the launch traced here: 134 us
  waiting for transfers between devices  79.1 us (59%)
  starting transfers between devices  21 us (16%)
  local copies, waits for them, and re-layouts  16.1 us (12%)
  between operations  14.4 us (11%)
  other arithmetic  3.54 us (3%)
    reduce_scatter x1, waiting for transfers between devices, body(): lax.psum_scatter(local_terms, 'brick', scatter_dimension=1, tiled=True)  64.2 us
    unnamed x34, local copies, waits for them, and re-layouts  10.7 us
    ppermute x4, starting transfers between devices, padded(): before = lax.ppermute(last, axis, up)  9.21 us
    all_to_all x1, waiting for transfers between devices, body(): lax.all_to_all(jnp.stack(jnp.split(jac_blocks, lax.axis_size('brick'), ax...  8.77 us
    all_to_all x1, starting transfers between devices, body(): lax.all_to_all(jnp.stack(jnp.split(jac_blocks, lax.axis_size('brick'), ax...  7.96 us
    split x1, local copies, waits for them, and re-layouts, body(): jnp.split(jac_blocks, lax.axis_size('brick'), axis=2)  3.97 us
    ppermute x4, starting transfers between devices, padded(): after = lax.ppermute(initial, axis, down)  3.79 us
    ppermute x4, waiting for transfers between devices, padded(): before = lax.ppermute(last, axis, up)  3.08 us
  transfers between devices with their start and end apart: 10, of which 6 were waited for; matrix products, arithmetic and copies ran while one was open for 10% of the time, Pallas kernels for 0%

profile of v1, /device:TPU:0, one launch (start us, length us, event | category | flops | bytes accessed | tf_op | source)
XLA Modules:
  0.0 134.2 jit_solution(520305879179206095)
XLA Ops:
  7.2 1.4 %collective-permute-start = (f32[1,10,1,64,128]{4,3,1,2,0:T(8,128)}, f32[1,10,1,64,128]{4,3,1,2,0:T(8,128)S(1)}, u32[]{:S(2)}, u32[]{:S(2)}) collective-permute-start(f32[1,10,1,64,128]{4,3,1,2,0:T(8,128)} %bitcast.138), channel_id=1, source_target_pairs={{1,0},{2,1},{3,2},{4,3},{5,4},{6,5},{7,6},{8,7},{9,8},{10,9},{11,1... | collective-permute-start | bytes 983048 | tf_op jit(solution)/shard_map/ppermute | solution.py:21
  8.6 3.0 %collective-permute-start.1 = (f32[1,10,1,64,128]{4,3,1,2,0:T(8,128)}, f32[1,10,1,64,128]{4,3,1,2,0:T(8,128)S(1)}, u32[]{:S(2)}, u32[]{:S(2)}) collective-permute-start(f32[1,10,1,64,128]{4,3,1,2,0:T(8,128)} %bitcast.139), channel_id=1, source_target_pairs={{0,1},{1,2},{2,3},{3,4},{4,5},{5,6},{6,7},{7,8},{8,9},{9,10},{10,1... | collective-permute-start | bytes 983048 | tf_op jit(solution)/shard_map/ppermute | solution.py:20
  11.7 4.0 %fusion.52 = (bf16[1,25,1,512]{3,2,1,0:T(2,128)(2,1)S(1)}, bf16[1,25,1,512]{3,2,1,0:T(2,128)(2,1)S(1)}, bf16[1,25,1,512]{3,2,1,0:T(2,128)(2,1)S(1)}, bf16[1,25,1...) fusion(bf16[1,25,16,512]{3,2,1,0:T(8,128)(2,1)} %param.9), kind=kLoop, calls=%fused_computation.181 | loop fusion | bytes 819200 | tf_op jit(solution)/shard_map/split | solution.py:96
  15.7 0.0 copy-start.8
  15.7 0.6 constant_dynamic-update-slice_fusion.15
  16.3 0.6 constant_dynamic-update-slice_fusion.14
  16.9 0.6 constant_dynamic-update-slice_fusion.13
  17.5 0.6 constant_dynamic-update-slice_fusion.12
  18.1 0.6 constant_dynamic-update-slice_fusion.11
  18.7 0.6 constant_dynamic-update-slice_fusion.10
  19.3 0.6 constant_dynamic-update-slice_fusion.9
  19.9 0.6 constant_dynamic-update-slice_fusion.8
  20.5 0.6 constant_dynamic-update-slice_fusion.7
  21.2 0.6 constant_dynamic-update-slice_fusion.6
  21.8 0.6 constant_dynamic-update-slice_fusion.5
  22.4 0.6 constant_dynamic-update-slice_fusion.4
  23.0 0.6 constant_dynamic-update-slice_fusion.3
  23.6 0.6 constant_dynamic-update-slice_fusion.2
  24.2 0.6 constant_dynamic-update-slice_fusion.1
  24.8 0.6 constant_dynamic-update-slice_fusion
  25.4 8.0 %all-to-all-start = ((bf16[16,1,25,1,512]{4,2,3,1,0:T(8,128)(2,1)}), bf16[16,1,25,1,512]{4,2,3,1,0:T(8,128)(2,1)S(1)}, u32[]{:S(2)}, u32[]{:S(2)}) async-start(bf16[16,1,25,1,512]{4,2,3,1,0:T(8,128)(2,1)} %constant_dynamic-update-slice_fusion), calls=%async_computation | async-start | bytes 1048576 | tf_op jit(solution)/shard_map/all_to_all | solution.py:95
  33.4 0.0 reduce-scatter.2.cloned.1.call-start
  33.5 1.6 %collective-permute-start.2 = (bf16[1,10,1,1,128]{4,3,1,2,0:T(2,128)(2,1)S(1)}, bf16[1,10,1,1,128]{4,3,1,2,0:T(2,128)(2,1)S(1)}, u32[]{:S(2)}, u32[]{:S(2)}) collective-permute-start(bf16[1,10,1,1,128]{4,3,1,2,0:T(2,128)(2,1)S(1)} %get-tuple-element.78), channel_id=1, source_target_pairs={{0,16},{16,0},{1,17},{17,1},{2,18},{18,2},{3,19},{19,3},{4,20},{20... | collective-permute-start | bytes 7688 | tf_op jit(solution)/shard_map/ppermute | solution.py:20
  35.0 0.5 collective-permute-start.3
  35.7 1.5 %collective-permute-done.2 = bf16[1,10,1,1,128]{4,3,1,2,0:T(2,128)(2,1)S(1)} collective-permute-done((bf16[1,10,1,1,128]{4,3,1,2,0:T(2,128)(2,1)S(1)}, bf16[1,10,1,1,128]{4,3,1,2,0:T(2,128)(2,1)S(1)}, u32[]{:S(2)}, u32[]{:S(2)}) %collective-permute-start.2) | collective-permute-done | bytes 2592 | tf_op jit(solution)/shard_map/ppermute | solution.py:20
  37.2 1.5 %collective-permute-done.3 = bf16[1,10,1,1,128]{4,3,1,2,0:T(2,128)(2,1)S(1)} collective-permute-done((bf16[1,10,1,1,128]{4,3,1,2,0:T(2,128)(2,1)S(1)}, bf16[1,10,1,1,128]{4,3,1,2,0:T(2,128)(2,1)S(1)}, u32[]{:S(2)}, u32[]{:S(2)}) %collective-permute-start.3) | collective-permute-done | bytes 2592 | tf_op jit(solution)/shard_map/ppermute | solution.py:21
  38.9 8.8 %all-to-all-done = bf16[16,1,25,1,512]{4,2,3,1,0:T(8,128)(2,1)S(1)} async-done(((bf16[16,1,25,1,512]{4,2,3,1,0:T(8,128)(2,1)}), bf16[16,1,25,1,512]{4,2,3,1,0:T(8,128)(2,1)S(1)}, u32[]{:S(2)}, u32[]{:S(2)}) %all-to-all-start) | async-done | bytes 409632 | tf_op jit(solution)/shard_map/all_to_all | solution.py:95
  47.6 0.2 copy.116
  47.9 0.2 reshape_reshape.3
  48.1 0.1 fusion.25
  48.2 0.1 fusion.29
  48.4 0.3 fusion.50
  48.7 1.3 collective-permute-start.4
  50.0 3.1 %collective-permute-start.5 = (f32[1,10,1,64,128]{4,3,1,2,0:T(8,128)S(1)}, f32[1,10,1,64,128]{4,3,1,2,0:T(8,128)S(1)}, u32[]{:S(2)}, u32[]{:S(2)}) collective-permute-start(f32[1,10,1,64,128]{4,3,1,2,0:T(8,128)S(1)} %get-tuple-element.19), channel_id=1, source_target_pairs={{0,1},{1,2},{2,3},{3,4},{4,5},{5,6},{6,7},{7,8},{8,9},{9,10},{10,1... | collective-permute-start | bytes 983048 | tf_op jit(solution)/shard_map/ppermute | solution.py:20
  53.1 1.6 %collective-permute-start.6 = (bf16[1,10,1,1,128]{4,3,1,2,0:T(2,128)(2,1)S(1)}, bf16[1,10,1,1,128]{4,3,1,2,0:T(2,128)(2,1)S(1)}, u32[]{:S(2)}, u32[]{:S(2)}) collective-permute-start(bf16[1,10,1,1,128]{4,3,1,2,0:T(2,128)(2,1)S(1)} %get-tuple-element.76), channel_id=1, source_target_pairs={{0,16},{16,0},{1,17},{17,1},{2,18},{18,2},{3,19},{19,3},{4,20},{20... | collective-permute-start | bytes 7688 | tf_op jit(solution)/shard_map/ppermute | solution.py:20
  54.6 0.5 collective-permute-start.7
  55.2 1.6 %collective-permute-done.6 = bf16[1,10,1,1,128]{4,3,1,2,0:T(2,128)(2,1)S(1)} collective-permute-done((bf16[1,10,1,1,128]{4,3,1,2,0:T(2,128)(2,1)S(1)}, bf16[1,10,1,1,128]{4,3,1,2,0:T(2,128)(2,1)S(1)}, u32[]{:S(2)}, u32[]{:S(2)}) %collective-permute-start.6) | collective-permute-done | bytes 2592 | tf_op jit(solution)/shard_map/ppermute | solution.py:20
  56.7 1.5 %collective-permute-done.7 = bf16[1,10,1,1,128]{4,3,1,2,0:T(2,128)(2,1)S(1)} collective-permute-done((bf16[1,10,1,1,128]{4,3,1,2,0:T(2,128)(2,1)S(1)}, bf16[1,10,1,1,128]{4,3,1,2,0:T(2,128)(2,1)S(1)}, u32[]{:S(2)}, u32[]{:S(2)}) %collective-permute-start.7) | collective-permute-done | bytes 2592 | tf_op jit(solution)/shard_map/ppermute | solution.py:21
  58.4 0.1 fusion.33
  58.5 0.1 fusion.37
  58.6 0.4 fusion.17
  59.0 0.0 copy-start.2
  59.0 0.1 slice_reduce_fusion.1
  59.2 0.1 copy.149
  59.3 2.2 %scatter_custom_fusion = f32[6,4096]{0,1:T(8,128)} fusion(s32[64]{0:T(128)S(1)} %fusion.49, f32[]{:T(128)} %constant.11.clone.1, f32[6,1,64]{0,2,1:T(8,128)S(1)} %copy.149), kind=kCustom, calls=%fused_computation.1 | custom fusion | flops 384 | bytes 131076 | tf_op jit(solution)/shard_map/scatter-add | solution.py:127
  61.5 0.0 reduce-scatter.2.cloned.1.call-update
  61.5 64.2 %reduce-scatter.2.cloned.1.call-done = f32[6,256]{0,1:T(8,128)} async-done(((f32[6,4096]{0,1:T(8,128)}), f32[6,256]{0,1:T(8,128)}) %reduce-scatter.2.cloned.1.call-update) | async-done | bytes 6160 | tf_op jit(solution)/shard_map/reduce_scatter | solution.py:128
  125.7 1.6 %copy.131 = f32[1,6,256]{2,0,1:T(1,128)} copy(f32[1,6,256]{1,2,0:T(8,128)} %bitcast.150) | data formatting | bytes 12288
  (40 shorter events, 0.4 us)
Async XLA Ops:
  7.2 26.3 %copy-start = (f32[1,10,1,64,128]{4,3,2,1,0:T(8,128)S(1)}, f32[1,10,1,64,128]{4,3,2,1,0:T(8,128)}, u32[]{:S(2)}) copy-start(f32[1,10,1,64,128]{4,3,2,1,0:T(8,128)} %param.10) | copy-start | bytes 983044
  7.2 28.4 %copy-start.3 = (f32[1,1,64,128]{3,2,1,0:T(8,128)S(1)}, f32[1,1,64,128]{3,2,1,0:T(8,128)}, u32[]{:S(2)}) copy-start(f32[1,1,64,128]{3,2,1,0:T(8,128)} %param.14) | copy-start | bytes 98308
  7.2 31.6 %collective-permute-start = (f32[1,10,1,64,128]{4,3,1,2,0:T(8,128)}, f32[1,10,1,64,128]{4,3,1,2,0:T(8,128)S(1)}, u32[]{:S(2)}, u32[]{:S(2)}) collective-permute-start(f32[1,10,1,64,128]{4,3,1,2,0:T(8,128)} %bitcast.138), channel_id=1, source_target_pairs={{1,0},{2,1},{3,2},{4,3},{5,4},{6,5},{7,6},{8,7},{9,8},{10,9},{11,1... | collective-permute-start | bytes 983048 | tf_op jit(solution)/shard_map/ppermute | solution.py:21
  8.6 30.1 %collective-permute-start.1 = (f32[1,10,1,64,128]{4,3,1,2,0:T(8,128)}, f32[1,10,1,64,128]{4,3,1,2,0:T(8,128)S(1)}, u32[]{:S(2)}, u32[]{:S(2)}) collective-permute-start(f32[1,10,1,64,128]{4,3,1,2,0:T(8,128)} %bitcast.139), channel_id=1, source_target_pairs={{0,1},{1,2},{2,3},{3,4},{4,5},{5,6},{6,7},{7,8},{8,9},{9,10},{10,1... | collective-permute-start | bytes 983048 | tf_op jit(solution)/shard_map/ppermute | solution.py:20
  15.7 20.0 %copy-start.7 = (s32[1,64]{1,0:T(1,128)S(1)}, s32[1,64]{1,0:T(1,128)}, u32[]{:S(2)}) copy-start(s32[1,64]{1,0:T(1,128)} %param.17) | copy-start | bytes 772
  15.7 20.0 %copy-start.8 = (s32[1,64,1]{1,2,0:T(1,128)S(1)}, s32[1,64,1]{1,2,0:T(1,128)}, u32[]{:S(2)}) copy-start(s32[1,64,1]{1,2,0:T(1,128)} %param.16) | copy-start | bytes 772
  25.4 22.2 %all-to-all-start = ((bf16[16,1,25,1,512]{4,2,3,1,0:T(8,128)(2,1)}), bf16[16,1,25,1,512]{4,2,3,1,0:T(8,128)(2,1)S(1)}, u32[]{:S(2)}, u32[]{:S(2)}) async-start(bf16[16,1,25,1,512]{4,2,3,1,0:T(8,128)(2,1)} %constant_dynamic-update-slice_fusion), calls=%async_computation | async-start | bytes 1048576 | tf_op jit(solution)/shard_map/all_to_all | solution.py:95
  33.4 92.4 %reduce-scatter.2.cloned.1.call-start = ((), (), s32[]{:S(2)}) async-start(), calls=%async_computation.2 | async-start | bytes 2228224 | tf_op jit(solution)/shard_map/reduce_scatter | solution.py:128
  33.5 3.7 %collective-permute-start.2 = (bf16[1,10,1,1,128]{4,3,1,2,0:T(2,128)(2,1)S(1)}, bf16[1,10,1,1,128]{4,3,1,2,0:T(2,128)(2,1)S(1)}, u32[]{:S(2)}, u32[]{:S(2)}) collective-permute-start(bf16[1,10,1,1,128]{4,3,1,2,0:T(2,128)(2,1)S(1)} %get-tuple-element.78), channel_id=1, source_target_pairs={{0,16},{16,0},{1,17},{17,1},{2,18},{18,2},{3,19},{19,3},{4,20},{20... | collective-permute-start | bytes 7688 | tf_op jit(solution)/shard_map/ppermute | solution.py:20
  35.0 3.6 %collective-permute-start.3 = (bf16[1,10,1,1,128]{4,3,1,2,0:T(2,128)(2,1)S(1)}, bf16[1,10,1,1,128]{4,3,1,2,0:T(2,128)(2,1)S(1)}, u32[]{:S(2)}, u32[]{:S(2)}) collective-permute-start(bf16[1,10,1,1,128]{4,3,1,2,0:T(2,128)(2,1)S(1)} %get-tuple-element.79), channel_id=1, source_target_pairs={{16,0},{0,16},{17,1},{1,17},{18,2},{2,18},{19,3},{3,19},{20,4},{4,... | collective-permute-start | bytes 7688 | tf_op jit(solution)/shard_map/ppermute | solution.py:21
  38.8 9.5 %copy-start.1 = (f32[1,10,1,64,128]{4,3,2,1,0:T(8,128)S(1)}, f32[1,10,1,64,128]{4,3,2,1,0:T(8,128)}, u32[]{:S(2)}) copy-start(f32[1,10,1,64,128]{4,3,2,1,0:T(8,128)} %param.11) | copy-start | bytes 983044
  38.8 9.5 %copy-start.4 = (f32[1,1,64,128]{3,2,1,0:T(8,128)S(1)}, f32[1,1,64,128]{3,2,1,0:T(8,128)}, u32[]{:S(2)}) copy-start(f32[1,1,64,128]{3,2,1,0:T(8,128)} %param.13) | copy-start | bytes 98308
  38.8 9.5 %copy-start.5 = (f32[1,1,64,128]{3,2,1,0:T(8,128)S(1)}, f32[1,1,64,128]{3,2,1,0:T(8,128)}, u32[]{:S(2)}) copy-start(f32[1,1,64,128]{3,2,1,0:T(8,128)} %param.12) | copy-start | bytes 98308
  48.7 9.6 %collective-permute-start.4 = (f32[1,10,1,64,128]{4,3,1,2,0:T(8,128)S(1)}, f32[1,10,1,64,128]{4,3,1,2,0:T(8,128)S(1)}, u32[]{:S(2)}, u32[]{:S(2)}) collective-permute-start(f32[1,10,1,64,128]{4,3,1,2,0:T(8,128)S(1)} %get-tuple-element.19), channel_id=1, source_target_pairs={{1,0},{2,1},{3,2},{4,3},{5,4},{6,5},{7,6},{8,7},{9,8},{10,9},{11,1... | collective-permute-start | bytes 983048 | tf_op jit(solution)/shard_map/ppermute | solution.py:21
  50.0 8.4 %collective-permute-start.5 = (f32[1,10,1,64,128]{4,3,1,2,0:T(8,128)S(1)}, f32[1,10,1,64,128]{4,3,1,2,0:T(8,128)S(1)}, u32[]{:S(2)}, u32[]{:S(2)}) collective-permute-start(f32[1,10,1,64,128]{4,3,1,2,0:T(8,128)S(1)} %get-tuple-element.19), channel_id=1, source_target_pairs={{0,1},{1,2},{2,3},{3,4},{4,5},{5,6},{6,7},{7,8},{8,9},{9,10},{10,1... | collective-permute-start | bytes 983048 | tf_op jit(solution)/shard_map/ppermute | solution.py:20
  53.1 3.7 %collective-permute-start.6 = (bf16[1,10,1,1,128]{4,3,1,2,0:T(2,128)(2,1)S(1)}, bf16[1,10,1,1,128]{4,3,1,2,0:T(2,128)(2,1)S(1)}, u32[]{:S(2)}, u32[]{:S(2)}) collective-permute-start(bf16[1,10,1,1,128]{4,3,1,2,0:T(2,128)(2,1)S(1)} %get-tuple-element.76), channel_id=1, source_target_pairs={{0,16},{16,0},{1,17},{17,1},{2,18},{18,2},{3,19},{19,3},{4,20},{20... | collective-permute-start | bytes 7688 | tf_op jit(solution)/shard_map/ppermute | solution.py:20
  54.6 3.6 %collective-permute-start.7 = (bf16[1,10,1,1,128]{4,3,1,2,0:T(2,128)(2,1)S(1)}, bf16[1,10,1,1,128]{4,3,1,2,0:T(2,128)(2,1)S(1)}, u32[]{:S(2)}, u32[]{:S(2)}) collective-permute-start(bf16[1,10,1,1,128]{4,3,1,2,0:T(2,128)(2,1)S(1)} %get-tuple-element.77), channel_id=1, source_target_pairs={{16,0},{0,16},{17,1},{1,17},{18,2},{2,18},{19,3},{3,19},{20,4},{4,... | collective-permute-start | bytes 7688 | tf_op jit(solution)/shard_map/ppermute | solution.py:21
  58.4 0.7 copy-start.6
  59.0 2.5 %copy-start.2 = (f32[1,10,1,64,128]{4,3,1,2,0:T(8,128)}, f32[1,10,1,64,128]{4,3,1,2,0:T(8,128)S(1)}, u32[]{:S(2)}) copy-start(f32[1,10,1,64,128]{4,3,1,2,0:T(8,128)S(1)} %fusion.17) | copy-start | bytes 983044
Sparse Core Ops, SparseCore 0:
  61.6 64.0 reduce-scatter.1
